TPU v7x, 32 devices: a whole 2x2x4 slice. The times are simulated.
32 devices in a mesh: parts: 2 (over y), pair: 4 (over x, core), sub: 4 (over z).
Axes of the slice: x: 2, y: 2, z: 4, core: 2. Of those that a mesh axis runs over, the one named last changes fastest.
Arguments:
- features: bfloat16 [64, 1024, 256], P(('parts', 'pair'), 'sub'), parts along dimension 0, may hold values from -7 to 7
- counts: int32 [64], P('parts'), parts along dimension 0, may hold values from 256 to 1024
- pair_table: int32 [8, 4, 2], P('parts'), parts along dimension 0, may hold values from -1 to 31, as said below
- w_qk: bfloat16 [256, 256], replicated, may hold values from -0.75 to 0.75
- w_value: bfloat16 [256, 256], replicated, may hold values from -0.375 to 0.375
- w_out: bfloat16 [256, 256], replicated, may hold values from -1.5 to 1.5
- w_merge_in: bfloat16 [512, 512], replicated, may hold values from -0.25 to 0.25
- w_merge_out: bfloat16 [512, 256], replicated, may hold values from -0.25 to 0.25
Outputs:
- updated: bfloat16 [64, 1024, 256], P(('parts', 'pair'), 'sub'), parts along dimension 0
There are 2 independent parts, one for each index of `parts`. A program takes and returns all parts, laid end to end along the dimension named above; an argument that names none is the same for every part. Nothing has to cross between parts.
Inputs may be any that keep to these rules, and one draw needn't show every extreme that they name: `pair_table`: row g lists the pairs owned by index g of pair, one slot per index of sub; -1 in both entries marks an empty slot. A live slot names two images of different groups, image i belonging to group i // 8. Over the live slots of one owner, at most 2 named images (counted with repetition) belong to any one group; some owner has all 4 slots live and reaches that bound for every group.
All inputs are finite; a program needn't handle non-finite values.
Results may differ from a plain program's by a relative error of at most 0.0067.
Values may be sent and summed in bfloat16 or wider, within the bound.
A program may use at most 64 MiB of HBM per device.

v0:
```python
import jax
import jax.numpy as jnp
from jax import lax
from jax.sharding import PartitionSpec as P

HEADS = 4


ln_eps = 1e-05


def layer_norm(hidden):
    center = jnp.mean(hidden, axis=-1, keepdims=True)
    centered = hidden - center
    variance = jnp.mean(centered * centered, axis=-1, keepdims=True)
    return centered * lax.rsqrt(variance + ln_eps)


def pair_messages(left_feats, right_feats, left_count, right_count, w_qk, w_value, head_count):
    points = left_feats.shape[0]
    model_width = left_feats.shape[1]
    head_dim = model_width // head_count
    stacked = jnp.concatenate([left_feats, right_feats], axis=0)
    query_key = jnp.dot(stacked, w_qk, preferred_element_type=jnp.float32).astype(jnp.bfloat16)
    values = jnp.dot(stacked, w_value, preferred_element_type=jnp.float32).astype(jnp.bfloat16)
    row_ids = lax.broadcasted_iota(jnp.int32, (points, 1), 0)
    col_ids = lax.broadcasted_iota(jnp.int32, (1, points), 1)
    col_valid = col_ids < right_count
    row_valid = row_ids < left_count
    score_scale = head_dim ** (-0.5)
    to_left = []
    to_right = []
    for head_index in range(head_count):
        head_lo = head_index * head_dim
        q_left = query_key[:points, head_lo : head_lo + head_dim]
        q_right = query_key[points:, head_lo : head_lo + head_dim]
        v_left = values[:points, head_lo : head_lo + head_dim]
        v_right = values[points:, head_lo : head_lo + head_dim]
        scores = (
            lax.dot_general(
                q_left, q_right, (((1,), (1,)), ((), ())), preferred_element_type=jnp.float32
            )
            * score_scale
        )
        masked = jnp.where(col_valid, scores, -jnp.inf)
        row_top = jnp.max(masked, axis=1, keepdims=True)
        row_exp = jnp.exp(masked - row_top)
        row_total = jnp.sum(row_exp, axis=1, keepdims=True)
        to_left.append(
            jnp.dot(row_exp.astype(jnp.bfloat16), v_right, preferred_element_type=jnp.float32)
            / row_total
        )
        col_masked = jnp.where(row_valid, scores, -jnp.inf)
        col_top = jnp.max(col_masked, axis=0, keepdims=True)
        col_exp = jnp.exp(col_masked - col_top)
        col_total = jnp.sum(col_exp, axis=0, keepdims=True)
        summed = lax.dot_general(
            col_exp.astype(jnp.bfloat16),
            v_left,
            (((0,), (0,)), ((), ())),
            preferred_element_type=jnp.float32,
        )
        to_right.append(summed / col_total.reshape(points, 1))
    return (
        jnp.concatenate(to_left, axis=1).astype(jnp.bfloat16),
        jnp.concatenate(to_right, axis=1).astype(jnp.bfloat16),
    )


def local(features, counts, pair_table, w_qk, w_value, w_out, w_merge_in, w_merge_out):
    n_pair = lax.axis_size("pair")
    n_sub = lax.axis_size("sub")
    me_group = lax.axis_index("pair")
    me_sub = lax.axis_index("sub")
    img_grp, kp_block, model_width = features.shape
    per_src = 2 * n_sub // n_pair
    positions = 2 * n_sub
    slot_table = pair_table.reshape(n_pair, positions)
    slot_live = slot_table >= 0
    source = jnp.where(slot_live, slot_table // img_grp, -1)
    group_ids = jnp.arange(n_pair, dtype=jnp.int32)
    src_hot = (source[:, :, None] == group_ids[None, None, :]).astype(jnp.int32)
    src_rank = jnp.sum((jnp.cumsum(src_hot, axis=1) - 1) * src_hot, axis=2)
    src_rank = jnp.where(slot_live, src_rank, -1)
    slot_ids = jnp.arange(per_src, dtype=jnp.int32)
    from_me = source == me_group
    send_match = from_me[:, None, :] & (src_rank[:, None, :] == slot_ids[None, :, None])
    send_local = jnp.sum(
        jnp.where(send_match, slot_table[:, None, :] - me_group * img_grp, 0), axis=2
    )
    send_ok = jnp.any(send_match, axis=2)
    my_table = lax.dynamic_index_in_dim(slot_table, me_group, 0, keepdims=False)
    my_live = lax.dynamic_index_in_dim(slot_live, me_group, 0, keepdims=False)
    my_source = lax.dynamic_index_in_dim(source, me_group, 0, keepdims=False)
    my_rank = lax.dynamic_index_in_dim(src_rank, me_group, 0, keepdims=False)
    outgoing = jnp.take(features, send_local.reshape(-1), axis=0).reshape(
        n_pair, per_src, kp_block, model_width
    )
    outgoing = jnp.where(send_ok[:, :, None, None], outgoing, jnp.zeros_like(outgoing))
    arrived = lax.all_to_all(outgoing, "pair", split_axis=0, concat_axis=0, tiled=True)
    flat_index = jnp.maximum(my_source * per_src + my_rank, 0)
    picked = jnp.take(arrived.reshape(n_pair * per_src, kp_block, model_width), flat_index, axis=0)
    picked = jnp.where(my_live[:, None, None], picked, jnp.zeros_like(picked))
    grouped = picked.reshape(n_sub, 2, kp_block, model_width)
    pair_rows = lax.all_to_all(grouped, "sub", split_axis=0, concat_axis=2, tiled=True)
    slot_pair = jnp.maximum(lax.dynamic_slice_in_dim(my_table, 2 * me_sub, 2), 0)
    pair_counts = jnp.take(counts, slot_pair)
    to_left, to_right = pair_messages(
        pair_rows[0, 0], pair_rows[0, 1], pair_counts[0], pair_counts[1], w_qk, w_value, HEADS
    )
    outbound = jnp.stack([to_left, to_right], axis=0)[None]
    returned = lax.all_to_all(outbound, "sub", split_axis=2, concat_axis=0, tiled=True)
    returned = returned.reshape(positions, kp_block, model_width)
    returned = jnp.where(my_live[:, None, None], returned, jnp.zeros_like(returned))
    position_ids = jnp.arange(positions, dtype=jnp.int32)
    inverse = (
        (my_source[None, None, :] == group_ids[:, None, None])
        & (my_rank[None, None, :] == slot_ids[None, :, None])
        & my_live[None, None, :]
    )
    inv_pos = jnp.sum(jnp.where(inverse, position_ids[None, None, :], 0), axis=2)
    inv_ok = jnp.any(inverse, axis=2)
    homeward = jnp.take(returned, inv_pos.reshape(-1), axis=0).reshape(
        n_pair, per_src, kp_block, model_width
    )
    homeward = jnp.where(inv_ok[:, :, None, None], homeward, jnp.zeros_like(homeward))
    home_msgs = lax.all_to_all(homeward, "pair", split_axis=0, concat_axis=0, tiled=True)
    local_ids = jnp.arange(img_grp, dtype=jnp.int32)
    owner_hot = ((send_local.reshape(1, -1) == local_ids[:, None]) & send_ok.reshape(1, -1)).astype(
        jnp.bfloat16
    )
    msg_total = jnp.dot(
        owner_hot,
        home_msgs.reshape(n_pair * per_src, kp_block * model_width),
        preferred_element_type=jnp.float32,
    )
    global_ids = me_group * img_grp + local_ids
    use_count = jnp.sum(
        (pair_table.reshape(1, -1) == global_ids[:, None]).astype(jnp.int32), axis=1
    )
    divisor = jnp.maximum(use_count, 1).astype(jnp.float32)
    mean_msg = (msg_total / divisor[:, None]).astype(jnp.bfloat16)
    own_rows = features.reshape(-1, model_width)
    lifted = jnp.dot(
        mean_msg.reshape(-1, model_width), w_out, preferred_element_type=jnp.float32
    ).astype(jnp.bfloat16)
    hidden = jnp.dot(own_rows, w_merge_in[:model_width], preferred_element_type=jnp.float32)
    hidden = hidden + jnp.dot(lifted, w_merge_in[model_width:], preferred_element_type=jnp.float32)
    active = jax.nn.gelu(layer_norm(hidden), approximate=False).astype(jnp.bfloat16)
    updated = own_rows.astype(jnp.float32) + jnp.dot(
        active, w_merge_out, preferred_element_type=jnp.float32
    )
    return updated.astype(jnp.bfloat16).reshape(img_grp, kp_block, model_width)


def solution(mesh):
    in_specs = (
        P(("parts", "pair"), "sub", None),
        P("parts"),
        P("parts", None, None),
        P(),
        P(),
        P(),
        P(),
        P(),
    )
    out_specs = P(("parts", "pair"), "sub", None)
    return jax.shard_map(local, mesh=mesh, in_specs=in_specs, out_specs=out_specs, check_vma=False)
```

profile of v0, /device:TPU:0, one launch (start us, length us, event | category | flops | bytes accessed | tf_op | source)
XLA Modules:
  0.0 154.1 jit_solution(910745184698559716)
XLA Ops:
  0.0 0.8 copy.48
  2.8 1.8 %gather_fusion.1 = bf16[8,256,256]{2,1,0:T(8,128)(2,1)S(1)} fusion(bf16[8,256,256]{2,1,0:T(8,128)(2,1)} %param.10, s32[1024]{0:T(1024)S(1)} %pad_clamp_fusion.2), kind=kCustom, calls=%fused_computation.clone | custom fusion | bytes 2097184 | tf_op jit(solution)/shard_map/jit(_take)/gather | solution.py:96
  4.8 1.1 broadcast_select_fusion.2
  5.9 4.4 %all-to-all-start = ((bf16[4,2,256,256]{3,2,1,0:T(8,128)(2,1)}), bf16[4,2,256,256]{3,2,1,0:T(8,128)(2,1)S(1)}, u32[]{:S(2)}, u32[]{:S(2)}) async-start(bf16[4,2,256,256]{3,2,1,0:T(8,128)(2,1)} %broadcast_select_fusion.2), calls=%async_computation | async-start | bytes 2097152 | tf_op jit(solution)/shard_map/all_to_all | solution.py:100
  10.3 14.4 %all-to-all-done = bf16[4,2,256,256]{3,2,1,0:T(8,128)(2,1)S(1)} async-done(((bf16[4,2,256,256]{3,2,1,0:T(8,128)(2,1)}), bf16[4,2,256,256]{3,2,1,0:T(8,128)(2,1)S(1)}, u32[]{:S(2)}, u32[]{:S(2)}) %all-to-all-start) | async-done | bytes 1048608 | tf_op jit(solution)/shard_map/all_to_all | solution.py:100
  25.4 1.2 select_select_fusion
  26.5 5.6 %all-to-all-start.1 = ((bf16[4,2,256,256]{3,2,1,0:T(8,128)(2,1)}), bf16[4,2,256,256]{3,2,1,0:T(8,128)(2,1)S(1)}, u32[]{:S(2)}, u32[]{:S(2)}) async-start(bf16[4,2,256,256]{3,2,1,0:T(8,128)(2,1)} %bitcast.8), calls=%async_computation.1 | async-start | bytes 2097152 | tf_op jit(solution)/shard_map/all_to_all | solution.py:105
  33.8 1.3 iota_compare_fusion.1
  35.0 22.5 %all-to-all-done.1 = bf16[4,2,256,256]{3,2,1,0:T(8,128)(2,1)S(1)} async-done(((bf16[4,2,256,256]{3,2,1,0:T(8,128)(2,1)}), bf16[4,2,256,256]{3,2,1,0:T(8,128)(2,1)S(1)}, u32[]{:S(2)}, u32[]{:S(2)}) %all-to-all-start.1) | async-done | bytes 1048608 | tf_op jit(solution)/shard_map/all_to_all | solution.py:105
  58.2 0.7 fusion.141
  59.7 0.7 fusion.133
  60.9 1.9 %select_reduce_fusion.7 = (f32[1024]{0:T(1024)S(1)}, f32[1024]{0:T(1024)S(1)}, f32[1024]{0:T(1024)S(1)}, f32[1024]{0:T(1024)S(1)}, f32[1024,1024]{1,0:T(8,128)S(1)}) fusion(pred[1024]{0:T(1024)(128)(4,1)S(1)} %get-tuple-element.47, f32[1024,1024]{1,0:T(8,128)S(1)} %fusion.141, f32[1024,1024]{1,0:T(8,128)S(1)} %fusion.137, f32[1024,1024]{1,0:T(8,128)S(1)} %fusion.133, ...), kind=kOutput, calls=%fused_computation.41 | convolution fusion | flops 146796544 | bytes 17056768 | tf_op jit(solution)/shard_map/dot_general | solution.py:40
  62.8 6.2 %fusion.17 = (f32[1024]{0:T(1024)S(1)}, f32[1024]{0:T(1024)S(1)}, f32[1024]{0:T(1024)S(1)}, f32[1024]{0:T(1024)S(1)}, f32[1024]{0:T(1024)S(1)}, /*index=5*/f32[1024]{0:T(1024)S(1)}, f32[1024]{0:T(1024)S(1)}, f32[1024]{0:T(1024)S(1)}) fusion(f32[1024,1024]{1,0:T(8,128)S(1)} %fusion.133, f32[1024]{0:T(1024)S(1)} %get-tuple-element.23, ...), kind=kLoop, calls=%fused_computation.48 | loop fusion | flops 25157632 | bytes 16828416 | tf_op jit(solution)/shard_map/reduce_sum | solution.py:48
  69.0 4.2 %fusion.19 = (f32[1024]{0:T(1024)S(1)}, f32[1024]{0:T(1024)S(1)}, f32[1024]{0:T(1024)S(1)}, f32[1024]{0:T(1024)S(1)}) fusion(f32[1024,1024]{1,0:T(8,128)S(1)} %get-tuple-element.39, f32[1024]{0:T(1024)S(1)} %get-tuple-element.14, pred[1024]{0:T(1024)(128)(4,1)S(1)} %get-tuple-element.46, f32[1024]{0:T(1024)S(1)} %get-tuple-element.16, ...), kind=kLoop, calls=%fused_computation.50 | loop fusion | flops 16773120 | bytes 16811008 | tf_op jit(solution)/shard_map/reduce_sum | solution.py:56
  73.2 1.1 fusion.95
  74.3 1.0 fusion.59
  75.4 1.1 fusion.122
  76.5 1.0 fusion.86
  77.6 1.1 fusion.113
  78.7 1.0 fusion.77
  79.8 1.0 fusion.68
  80.8 1.1 fusion.104
  82.0 2.0 %copy.61 = bf16[1,2,1024,256]{3,1,0,2:T(2,128)(2,1)} copy(bf16[1,2,1024,256]{2,3,1,0:T(8,128)(2,1)S(1)} %maximum_bitcast_fusion) | data formatting | bytes 2097152 | tf_op jit(solution)/shard_map/broadcast_in_dim | solution.py:111
  84.1 3.5 %all-to-all-start.2 = ((bf16[1,2,1024,256]{3,1,0,2:T(2,128)(2,1)}), bf16[1,2,1024,256]{3,1,0,2:T(2,128)(2,1)S(1)}, u32[]{:S(2)}, u32[]{:S(2)}) async-start(bf16[1,2,1024,256]{3,1,0,2:T(2,128)(2,1)} %copy.61), calls=%async_computation.2 | async-start | bytes 2097152 | tf_op jit(solution)/shard_map/all_to_all | solution.py:112
  88.2 24.7 %all-to-all-done.2 = bf16[1,2,1024,256]{3,1,0,2:T(2,128)(2,1)S(1)} async-done(((bf16[1,2,1024,256]{3,1,0,2:T(2,128)(2,1)}), bf16[1,2,1024,256]{3,1,0,2:T(2,128)(2,1)S(1)}, u32[]{:S(2)}, u32[]{:S(2)}) %all-to-all-start.2) | async-done | bytes 1048608 | tf_op jit(solution)/shard_map/all_to_all | solution.py:112
  114.0 1.1 broadcast_select_fusion.3
  115.1 3.7 %all-to-all-start.3 = ((bf16[4,2,256,256]{3,2,1,0:T(8,128)(2,1)}), bf16[4,2,256,256]{3,2,1,0:T(8,128)(2,1)S(1)}, u32[]{:S(2)}, u32[]{:S(2)}) async-start(bf16[4,2,256,256]{3,2,1,0:T(8,128)(2,1)} %broadcast_select_fusion.3), calls=%async_computation.3 | async-start | bytes 2097152 | tf_op jit(solution)/shard_map/all_to_all | solution.py:127
  119.1 2.7 %fusion.126 = f32[2048,512]{0,1:T(8,128)} fusion(bf16[2048,256]{1,0:T(8,128)(2,1)S(1)} %bitcast.65, bf16[512,512]{1,0:T(8,128)(2,1)S(1)} %copy-done.4), kind=kOutput, calls=%fused_computation.115 | convolution fusion | flops 536870912 | bytes 5505024 | tf_op jit(solution)/shard_map/dot_general | solution.py:147
  121.8 11.3 %all-to-all-done.3 = bf16[4,2,256,256]{3,2,1,0:T(8,128)(2,1)S(1)} async-done(((bf16[4,2,256,256]{3,2,1,0:T(8,128)(2,1)}), bf16[4,2,256,256]{3,2,1,0:T(8,128)(2,1)S(1)}, u32[]{:S(2)}, u32[]{:S(2)}) %all-to-all-start.3) | async-done | bytes 1048608 | tf_op jit(solution)/shard_map/all_to_all | solution.py:127
  134.6 5.3 %fusion.214 = (f32[2048]{0:T(1024)S(1)}, f32[2048,512]{0,1:T(8,128)}) fusion(f32[2048,512]{0,1:T(8,128)} %fusion.126, bf16[512,512]{1,0:T(8,128)(2,1)} %param.16, bf16[2048,256]{1,0:T(8,128)(2,1)S(1)} %reshape.377, bf16[256,256]{1,0:T(8,128)(2,1)S(1)} %copy-done.5), kind=kOutput, calls=%fused_computation.240 | convolution fusion | flops 807925760 | bytes 9838592 | tf_op jit(solution)/shard_map/dot_general | solution.py:148
  139.9 2.8 %multiply_reduce_fusion = f32[2048]{0:T(1024)S(1)} fusion(f32[2048,512]{0,1:T(8,128)} %get-tuple-element.41, f32[2048]{0:T(1024)S(1)} %broadcast_multiply_fusion), kind=kLoop, calls=%fused_computation.23 | loop fusion | flops 3143680 | bytes 4210688 | tf_op jit(solution)/shard_map/reduce_sum | solution.py:15
  143.4 10.8 %fusion.27 = bf16[2048,256]{1,0:T(8,128)(2,1)} fusion(bf16[512,256]{1,0:T(8,128)(2,1)S(1)} %copy-done, bf16[2048,256]{1,0:T(8,128)(2,1)S(1)} %bitcast.66, f32[2048,512]{0,1:T(8,128)S(1)} %copy-done.2, f32[2048]{0:T(1024)S(1)} %add_rsqrt_fusion, f32[2048]{0:T(1024)S(1)} %broadcast_multiply_fusion), kind=kOutput, calls=%fused_computation.60 | convolution fusion | flops 608698368 | bytes 6569984 | tf_op jit(solution)/shard_map/dot_general | solution.py:150
  (75 shorter events, 10.3 us)
Async XLA Ops:
  0.0 142.7 %copy-start = (bf16[512,256]{1,0:T(8,128)(2,1)S(1)}, bf16[512,256]{1,0:T(8,128)(2,1)}, u32[]{:S(2)}) copy-start(bf16[512,256]{1,0:T(8,128)(2,1)} %param.17) | copy-start | bytes 786436
  5.9 26.4 %copy-start.1 = (s32[32]{0:T(128)S(1)}, s32[32]{0:T(128)}, u32[]{:S(2)}) copy-start(s32[32]{0:T(128)} %param.11) | copy-start | bytes 388
  5.9 18.8 %all-to-all-start = ((bf16[4,2,256,256]{3,2,1,0:T(8,128)(2,1)}), bf16[4,2,256,256]{3,2,1,0:T(8,128)(2,1)S(1)}, u32[]{:S(2)}, u32[]{:S(2)}) async-start(bf16[4,2,256,256]{3,2,1,0:T(8,128)(2,1)} %broadcast_select_fusion.2), calls=%async_computation | async-start | bytes 2097152 | tf_op jit(solution)/shard_map/all_to_all | solution.py:100
  25.4 32.4 %copy-start.7 = (bf16[256,256]{1,0:T(8,128)(2,1)S(1)}, bf16[256,256]{1,0:T(8,128)(2,1)}, u32[]{:S(2)}) copy-start(bf16[256,256]{1,0:T(8,128)(2,1)} %param.13) | copy-start | bytes 393220
  26.5 31.0 %all-to-all-start.1 = ((bf16[4,2,256,256]{3,2,1,0:T(8,128)(2,1)}), bf16[4,2,256,256]{3,2,1,0:T(8,128)(2,1)S(1)}, u32[]{:S(2)}, u32[]{:S(2)}) async-start(bf16[4,2,256,256]{3,2,1,0:T(8,128)(2,1)} %bitcast.8), calls=%async_computation.1 | async-start | bytes 2097152 | tf_op jit(solution)/shard_map/all_to_all | solution.py:105
  58.9 1.5 copy-start.8
  82.0 5.7 %copy-start.6 = (s32[4,4,2]{1,2,0:T(2,128)S(1)}, s32[4,4,2]{1,2,0:T(2,128)}, u32[]{:S(2)}) copy-start(s32[4,4,2]{1,2,0:T(2,128)} %param.12) | copy-start | bytes 388
  84.1 28.8 %all-to-all-start.2 = ((bf16[1,2,1024,256]{3,1,0,2:T(2,128)(2,1)}), bf16[1,2,1024,256]{3,1,0,2:T(2,128)(2,1)S(1)}, u32[]{:S(2)}, u32[]{:S(2)}) async-start(bf16[1,2,1024,256]{3,1,0,2:T(2,128)(2,1)} %copy.61), calls=%async_computation.2 | async-start | bytes 2097152 | tf_op jit(solution)/shard_map/all_to_all | solution.py:112
  113.2 5.9 %copy-start.3 = (bf16[8,256,256]{2,1,0:T(8,128)(2,1)S(1)}, bf16[8,256,256]{2,1,0:T(8,128)(2,1)}, u32[]{:S(2)}) copy-start(bf16[8,256,256]{2,1,0:T(8,128)(2,1)} %param.10) | copy-start | bytes 3145732
  113.9 5.3 %copy-start.4 = (bf16[512,512]{1,0:T(8,128)(2,1)S(1)}, bf16[512,512]{1,0:T(8,128)(2,1)}, u32[]{:S(2)}) copy-start(bf16[512,512]{1,0:T(8,128)(2,1)} %param.16) | copy-start | bytes 1572868
  115.1 17.9 %all-to-all-start.3 = ((bf16[4,2,256,256]{3,2,1,0:T(8,128)(2,1)}), bf16[4,2,256,256]{3,2,1,0:T(8,128)(2,1)S(1)}, u32[]{:S(2)}, u32[]{:S(2)}) async-start(bf16[4,2,256,256]{3,2,1,0:T(8,128)(2,1)} %broadcast_select_fusion.3), calls=%async_computation.3 | async-start | bytes 2097152 | tf_op jit(solution)/shard_map/all_to_all | solution.py:127
  133.7 0.9 copy-start.5
  139.9 3.4 %copy-start.2 = (f32[2048,512]{0,1:T(8,128)S(1)}, f32[2048,512]{0,1:T(8,128)}, u32[]{:S(2)}) copy-start(f32[2048,512]{0,1:T(8,128)} %get-tuple-element.41) | copy-start | bytes 12582916
where the time goes:
time: 155 us; the launch traced here: 154 us
  waiting for transfers between devices  72.9 us (47%)
  matrix products  33 us (21%)
  other arithmetic  20.4 us (13%)
  starting transfers between devices  17.2 us (11%)
  local copies, waits for them, and re-layouts  10.3 us (7%)
    all_to_all x1, waiting for transfers between devices, local(): lax.all_to_all(outbound, 'sub', split_axis=2, concat_axis=0, tiled=True)  24.7 us
    all_to_all x1, waiting for transfers between devices, local(): lax.all_to_all(grouped, 'sub', split_axis=0, concat_axis=2, tiled=True)  22.5 us
    all_to_all x1, waiting for transfers between devices, local(): lax.all_to_all(outgoing, 'pair', split_axis=0, concat_axis=0, tiled=True)  14.4 us
    all_to_all x1, waiting for transfers between devices, local(): lax.all_to_all(homeward, 'pair', split_axis=0, concat_axis=0, tiled=True)  11.3 us
    dot_general x1, matrix products, local(): jnp.dot(active, w_merge_out, preferred_element_type=jnp.float32)  10.8 us
    reduce_sum x1, other arithmetic, pair_messages(): row_total = jnp.sum(row_exp, axis=1, keepdims=True)  6.18 us
    all_to_all x1, starting transfers between devices, local(): lax.all_to_all(grouped, 'sub', split_axis=0, concat_axis=2, tiled=True)  5.6 us
    dot_general x1, matrix products, local(): jnp.dot(lifted, w_merge_in[model_width:], preferred_element_type=jnp.floa...  5.34 us
  transfers between devices with their start and end apart: 4, of which 4 were waited for; matrix products, arithmetic and copies ran while one was open for 4% of the time, Pallas kernels for 0%

commit v1 on v0

v1 whole, which is shorter than its diff:
```python
import functools

import jax
import jax.numpy as jnp
from jax import lax
from jax.experimental import pallas as pl
from jax.experimental.pallas import tpu as pltpu
from jax.sharding import PartitionSpec as P

HEADS = 4
SLAB = 128
CHUNKS = 2
MESH = pl.DeviceIdType.MESH

ln_eps = 1e-05


def partner(me, step, n):
    if n & (n - 1):
        return lax.rem(me + step, n)
    peer = 0
    bit = 1
    while bit < n:
        mine = (me // bit) % 2
        peer = peer + ((mine + (step // bit) % 2) % 2) * bit
        bit *= 2
    return peer


def source(me, step, n):
    if n & (n - 1):
        return lax.rem(me + n - step, n)
    return partner(me, step, n)


def exchange_kernel(
    dims, idx_ref, feat_ref, wqk_ref, wv_ref, home_ref, *scratch
):
    n_pair, n_sub, per_src, chunks, slabs, head_dim, tile = dims
    img_grp, kp, width = feat_ref.shape
    positions = 2 * n_sub
    sources = n_pair * per_src
    points = n_sub * kp
    scratch = list(scratch)
    send1 = scratch.pop(0)
    send2 = scratch.pop(0)
    rows_in = scratch.pop(0)
    qk = scratch.pop(0)
    vx = scratch.pop(0)
    msg = scratch.pop(0)
    hsend = scratch.pop(0)
    arrived = [scratch.pop(0) for _ in range(chunks)]
    returned = [scratch.pop(0) for _ in range(slabs)]
    s1, r1, s2, r2, s3, r3, s4, r4 = scratch

    me_pair = lax.axis_index("pair")
    me_sub = lax.axis_index("sub")
    part = kp // chunks

    barrier = pltpu.get_barrier_semaphore()
    for step in range(1, n_pair):
        pl.semaphore_signal(
            barrier, inc=1, device_id={"pair": partner(me_pair, step, n_pair)}, device_id_type=MESH
        )
    for step in range(1, n_sub):
        pl.semaphore_signal(
            barrier, inc=1, device_id={"sub": partner(me_sub, step, n_sub)}, device_id_type=MESH
        )
    pl.semaphore_wait(barrier, n_pair + n_sub - 2)

    waits = []
    pair_steps = list(range(n_pair - 1, 0, -1))
    sub_steps = list(range(n_sub - 1, 0, -1))

    phase1 = {}
    for c in range(chunks):
        rows = pl.ds(c * part, part)
        for step in pair_steps:
            peer = partner(me_pair, step, n_pair)
            for r in range(per_src):
                send1[step, r, rows, :] = feat_ref[idx_ref[peer * per_src + r], rows, :]
            copy = pltpu.make_async_remote_copy(
                src_ref=send1.at[step, :, rows, :],
                dst_ref=arrived[c].at[pl.ds(me_pair * per_src, per_src)],
                send_sem=s1.at[step, c],
                recv_sem=r1.at[step, c],
                device_id={"pair": peer},
                device_id_type=MESH,
            )
            copy.start()
            phase1[c, step] = copy
            waits.append(copy)
    for c in range(chunks):
        rows = pl.ds(c * part, part)
        for r in range(per_src):
            arrived[c][me_pair * per_src + r] = feat_ref[idx_ref[me_pair * per_src + r], rows, :]

    phase2 = {}
    for c in range(chunks):
        rows = pl.ds(c * part, part)
        for step in pair_steps:
            phase1[c, step].wait_recv()
        for step in sub_steps:
            peer = partner(me_sub, step, n_sub)
            for side in range(2):
                send2[step, side, rows, :] = arrived[c][idx_ref[sources + 2 * peer + side]]
            copy = pltpu.make_async_remote_copy(
                src_ref=send2.at[step, :, rows, :],
                dst_ref=rows_in.at[me_sub, :, rows, :],
                send_sem=s2.at[step, c],
                recv_sem=r2.at[step, c],
                device_id={"sub": peer},
                device_id_type=MESH,
            )
            copy.start()
            phase2[c, step] = copy
            waits.append(copy)
        for side in range(2):
            rows_in[me_sub, side, rows, :] = arrived[c][idx_ref[sources + 2 * me_sub + side]]

    ones = jnp.ones((kp, SLAB), jnp.bfloat16)

    def project(owner):
        for side in range(2):
            x = rows_in[owner, side]
            where = pl.ds(owner * kp, kp)
            q = jnp.dot(x, wqk_ref[...], preferred_element_type=jnp.float32)
            qk[side, where, :] = q.astype(jnp.bfloat16)
            v = jnp.dot(x, wv_ref[...], preferred_element_type=jnp.float32).astype(jnp.bfloat16)
            for slab in range(slabs):
                vx[side, slab, where, :SLAB] = v[:, slab * SLAB : (slab + 1) * SLAB]
                vx[side, slab, where, SLAB:] = ones

    project(me_sub)
    for step in reversed(sub_steps):
        for c in range(chunks):
            phase2[c, step].wait_recv()
        project(source(me_sub, step, n_sub))

    scale = head_dim ** (-0.5)
    in_slab = SLAB // head_dim
    tile_lane = lax.broadcasted_iota(jnp.int32, (tile, SLAB), 1) // head_dim
    col_ids = lax.broadcasted_iota(jnp.int32, (1, points), 1)
    base = sources + positions + sources

    def attend(side, slab):
        other = 1 - side
        valid = col_ids < idx_ref[base + other]
        columns = slice(slab * SLAB, (slab + 1) * SLAB)

        def body(t, carry):
            start = pl.multiple_of(t * tile, tile)
            q = qk[side, pl.ds(start, tile), columns] * jnp.asarray(scale, jnp.bfloat16)
            out = jnp.zeros((tile, SLAB), jnp.float32)
            for head in range(in_slab):
                mine = tile_lane == head
                qh = jnp.where(mine, q, jnp.zeros_like(q))
                sim = lax.dot_general(
                    qh,
                    qk[other, :, columns],
                    (((1,), (1,)), ((), ())),
                    preferred_element_type=jnp.float32,
                )
                sim = jnp.where(valid, sim, -jnp.inf)
                top = jnp.max(sim, axis=1, keepdims=True)
                weight = jnp.exp(sim - top).astype(jnp.bfloat16)
                both = jnp.dot(weight, vx[other, slab], preferred_element_type=jnp.float32)
                out = jnp.where(mine, both[:, :SLAB] / both[:, SLAB:], out)
            msg[slab, side, pl.ds(start, tile), :] = out.astype(jnp.bfloat16)
            return carry

        lax.fori_loop(0, points // tile, body, 0)

    phase3 = {}
    phase4 = {}

    def give_back(side, slab):
        for step in sub_steps:
            peer = partner(me_sub, step, n_sub)
            copy = pltpu.make_async_remote_copy(
                src_ref=msg.at[slab, side, pl.ds(peer * kp, kp), :],
                dst_ref=returned[slab].at[2 * me_sub + side],
                send_sem=s3.at[step, slab, side],
                recv_sem=r3.at[step, slab, side],
                device_id={"sub": peer},
                device_id_type=MESH,
            )
            copy.start()
            phase3[slab, side, step] = copy
            waits.append(copy)
        returned[slab][2 * me_sub + side] = msg[slab, side, pl.ds(me_sub * kp, kp), :]

    def send_home(slab):
        for side in range(2):
            for step in sub_steps:
                phase3[slab, side, step].wait_recv()
        first = sources + positions
        for step in pair_steps:
            peer = partner(me_pair, step, n_pair)
            for r in range(per_src):
                hsend[slab, step, r] = returned[slab][idx_ref[first + peer * per_src + r]]
            copy = pltpu.make_async_remote_copy(
                src_ref=hsend.at[slab, step],
                dst_ref=home_ref.at[slab, pl.ds(me_pair * per_src, per_src)],
                send_sem=s4.at[step, slab],
                recv_sem=r4.at[step, slab],
                device_id={"pair": peer},
                device_id_type=MESH,
            )
            copy.start()
            phase4[slab, step] = copy
            waits.append(copy)
        for r in range(per_src):
            home_ref[slab, me_pair * per_src + r] = returned[slab][
                idx_ref[first + me_pair * per_src + r]
            ]

    for slab in range(slabs):
        for side in range(2):
            attend(side, slab)
            give_back(side, slab)
    for slab in range(slabs):
        send_home(slab)
    for copy in phase4.values():
        copy.wait_recv()
    for copy in waits:
        copy.wait_send()


def erf(x):
    x = jnp.clip(x, -3.832506856900711, 3.832506856900711)
    y = x * x
    top = jnp.float32(0.00022905065861350646)
    for c in (0.0034082910107109506, 0.050955695062380861, 0.18520832239976145, 1.128379143519084):
        top = top * y + jnp.float32(c)
    low = jnp.float32(-1.1791602954361697e-7)
    for c in (0.000023547966471313185, 0.0010179625278914885, 0.014070470171167667, 0.11098505178285362, 0.49746925110067538, 1.0):
        low = low * y + jnp.float32(c)
    return x * top / low


def update_kernel(dims, weight_ref, feat_ref, home_ref, wout_ref, wmi_ref, wmo_ref, out_ref):
    sources, slabs = dims
    image = pl.program_id(0)
    kp, width = out_ref.shape
    parts = []
    for slab in range(slabs):
        total = jnp.zeros((kp, SLAB), jnp.float32)
        for s in range(sources):
            total = total + home_ref[slab, s].astype(jnp.float32) * weight_ref[image, s]
        parts.append(total)
    mean = (jnp.concatenate(parts, axis=1) / weight_ref[image, sources]).astype(jnp.bfloat16)
    lifted = jnp.dot(mean, wout_ref[...], preferred_element_type=jnp.float32).astype(jnp.bfloat16)
    feat = feat_ref[...]
    hidden = jnp.dot(feat, wmi_ref[:width], preferred_element_type=jnp.float32)
    hidden = hidden + jnp.dot(lifted, wmi_ref[width:], preferred_element_type=jnp.float32)
    center = jnp.mean(hidden, axis=-1, keepdims=True)
    centered = hidden - center
    variance = jnp.mean(centered * centered, axis=-1, keepdims=True)
    normed = centered * lax.rsqrt(variance + ln_eps)
    active = (0.5 * normed * (1.0 + erf(normed * (0.5**0.5)))).astype(jnp.bfloat16)
    out = feat.astype(jnp.float32) + jnp.dot(
        active, wmo_ref[...], preferred_element_type=jnp.float32
    )
    out_ref[...] = out.astype(jnp.bfloat16)


def local(features, counts, pair_table, w_qk, w_value, w_out, w_merge_in, w_merge_out):
    n_pair = lax.axis_size("pair")
    n_sub = lax.axis_size("sub")
    me_group = lax.axis_index("pair")
    me_sub = lax.axis_index("sub")
    img_grp, kp, width = features.shape
    per_src = 2 * n_sub // n_pair
    positions = 2 * n_sub
    sources = n_pair * per_src
    slabs = width // SLAB
    head_dim = width // HEADS
    points = n_sub * kp

    table = pair_table.reshape(n_pair, positions)
    live = table >= 0
    group = jnp.where(live, table // img_grp, -1)
    place = jnp.arange(positions, dtype=jnp.int32)
    earlier = place[None, None, :] < place[None, :, None]
    rank = jnp.sum(
        ((group[:, None, :] == group[:, :, None]) & earlier).astype(jnp.int32), axis=2
    )
    slot_ids = jnp.arange(per_src, dtype=jnp.int32)
    match = (group == me_group)[:, None, :] & (rank[:, None, :] == slot_ids[None, :, None])
    send_local = jnp.sum(
        jnp.where(match, table[:, None, :] - me_group * img_grp, 0), axis=2
    ).reshape(-1)
    send_ok = jnp.any(match, axis=2).reshape(-1)
    mine = lax.dynamic_index_in_dim(table, me_group, 0, keepdims=False)
    my_group = lax.dynamic_index_in_dim(group, me_group, 0, keepdims=False)
    my_rank = lax.dynamic_index_in_dim(rank, me_group, 0, keepdims=False)
    pick = jnp.where(mine >= 0, my_group * per_src + my_rank, 0)
    flat_ids = jnp.arange(sources, dtype=jnp.int32)
    back = jnp.sum(
        jnp.where(
            (pick[None, :] == flat_ids[:, None]) & (mine >= 0)[None, :], place[None, :], 0
        ),
        axis=1,
    )
    slot = jnp.maximum(lax.dynamic_slice_in_dim(mine, 2 * me_sub, 2), 0)
    slot_counts = jnp.take(counts, slot)
    index = jnp.concatenate([send_local, pick, back, slot_counts]).astype(jnp.int32)
    local_ids = jnp.arange(img_grp, dtype=jnp.int32)
    hot = ((send_local[None, :] == local_ids[:, None]) & send_ok[None, :]).astype(jnp.float32)
    uses = jnp.maximum(jnp.sum(hot, axis=1, keepdims=True), 1.0)
    weights = jnp.concatenate([hot, uses], axis=1)

    tile = min(256, points)
    bf = jnp.bfloat16
    chunks = CHUNKS
    dma = pltpu.SemaphoreType.DMA
    vmem = pl.BlockSpec(memory_space=pltpu.VMEM)
    smem = pl.BlockSpec(memory_space=pltpu.SMEM)
    dims = (n_pair, n_sub, per_src, chunks, slabs, head_dim, tile)
    home = pl.pallas_call(
        functools.partial(exchange_kernel, dims),
        out_shape=jax.ShapeDtypeStruct((slabs, sources, kp, SLAB), bf),
        in_specs=[smem, vmem, vmem, vmem],
        out_specs=vmem,
        scratch_shapes=[
            pltpu.VMEM((n_pair, per_src, kp, width), bf),
            pltpu.VMEM((n_sub, 2, kp, width), bf),
            pltpu.VMEM((n_sub, 2, kp, width), bf),
            pltpu.VMEM((2, points, width), bf),
            pltpu.VMEM((2, slabs, points, 2 * SLAB), bf),
            pltpu.VMEM((slabs, 2, points, SLAB), bf),
            pltpu.VMEM((slabs, n_pair, per_src, kp, SLAB), bf),
        ]
        + [pltpu.VMEM((sources, kp // chunks, width), bf) for _ in range(chunks)]
        + [pltpu.VMEM((positions, kp, SLAB), bf) for _ in range(slabs)]
        + [dma((n_pair, chunks))] * 2
        + [dma((n_sub, chunks))] * 2
        + [dma((n_sub, slabs, 2))] * 2
        + [dma((n_pair, slabs))] * 2,
        compiler_params=pltpu.CompilerParams(
            collective_id=0, has_side_effects=True, vmem_limit_bytes=56 * 1024 * 1024
        ),
        name="exchange",
    )(index, features, w_qk, w_value)

    return pl.pallas_call(
        functools.partial(update_kernel, (sources, slabs)),
        grid=(img_grp,),
        out_shape=jax.ShapeDtypeStruct(features.shape, bf),
        in_specs=[
            smem,
            pl.BlockSpec((None, kp, width), lambda i: (i, 0, 0)),
            vmem,
            vmem,
            vmem,
            vmem,
        ],
        out_specs=pl.BlockSpec((None, kp, width), lambda i: (i, 0, 0)),
        name="update",
    )(weights, features, home, w_out, w_merge_in, w_merge_out)


def solution(mesh):
    in_specs = (
        P(("parts", "pair"), "sub", None),
        P("parts"),
        P("parts", None, None),
        P(),
        P(),
        P(),
        P(),
        P(),
    )
    out_specs = P(("parts", "pair"), "sub", None)
    return jax.shard_map(local, mesh=mesh, in_specs=in_specs, out_specs=out_specs, check_vma=False)
```

time: 155 us -> 89.9 us (0.58)
  Pallas kernels: 0 us -> 85.1 us
  waiting for transfers between devices: 72.9 us -> 0 us
  matrix products: 33 us -> 0 us
  other arithmetic: 20.4 us -> 2.45 us
  starting transfers between devices: 17.2 us -> 0 us
  local copies, waits for them, and re-layouts: 10.3 us -> 2.06 us
    pallas_call x0 -> x2, Pallas kernels: none -> 85.1 us  [the longest x1 72.2 us: local(): pl.pallas_call(functools.partial(exchange_kernel, dims), out_shape=jax.Sh...]
    all_to_all x4 -> x0, waiting for transfers between devices: 72.9 us -> none  [the longest x1 24.7 us: local(): lax.all_to_all(outbound, 'sub', split_axis=2, concat_axis=0, tiled=True)]
    dot_general x18 -> x0, matrix products: 33 us -> none  [the longest x1 10.8 us: local(): jnp.dot(active, w_merge_out, preferred_element_type=jnp.float32)]
    all_to_all x4 -> x0, starting transfers between devices: 17.2 us -> none  [the longest x1 5.6 us: local(): lax.all_to_all(grouped, 'sub', split_axis=0, concat_axis=2, tiled=True)]
    reduce_sum x7 -> x4, other arithmetic: 13.7 us -> 0.59 us  [the longest x1 0.21 us: local(): jnp.sum(((group[:, None, :] == group[:, :, None]) & earlier).astype(jnp.i...]
    select_n x9 -> x2, other arithmetic: 3.87 us -> 0.02 us  [the longest x1 0.01 us: local(): pick = jnp.where(mine >= 0, my_group * per_src + my_rank, 0)]
    gather x4 -> x1, local copies, waits for them, and re-layouts: 3.7 us -> 0.64 us  [local(): slot_counts = jnp.take(counts, slot)]
    broadcast_in_dim x1 -> x0, local copies, waits for them, and re-layouts: 2.04 us -> none  [local(): outbound = jnp.stack([to_left, to_right], axis=0)[None]]
  transfers between devices with their start and end apart: 4 -> 0, of which waited for: 4 -> 0; matrix products, arithmetic and copies ran while one was open for 4% -> 0% of each run, Pallas kernels for 0% -> 0%
where the time goes in v1:
time: 89.9 us; the launch traced here: 89.7 us
  Pallas kernels  85.1 us (95%)
  other arithmetic  2.45 us (3%)
  local copies, waits for them, and re-layouts  2.06 us (2%)
    pallas_call x1, Pallas kernels, local(): pl.pallas_call(functools.partial(exchange_kernel, dims), out_shape=jax.Sh...  72.2 us
    pallas_call x1, Pallas kernels, local(): pl.pallas_call(functools.partial(update_kernel, (sources, slabs)), grid=(...  12.8 us

profile of v1, /device:TPU:0, one launch (start us, length us, event | category | flops | bytes accessed | tf_op | source)
XLA Modules:
  0.0 89.7 jit_solution(3220683007497885062)
XLA Ops:
  0.0 0.0 copy-start
  0.0 0.0 copy-start.1
  0.0 0.7 copy-done.1
  0.7 0.1 copy.23
  0.8 0.2 fusion.12
  1.0 0.2 compare_reduce_fusion
  1.2 0.1 copy.24
  1.3 0.1 copy.29
  1.4 0.2 convert_reduce_fusion
  1.6 0.1 select_reduce_fusion.1
  1.8 0.2 fusion.4
  1.9 0.1 copy.31
  2.0 0.1 and.75
  2.1 0.1 select_reduce_fusion
  2.2 0.1 copy.30
  2.3 0.1 eq.72
  2.4 0.1 fusion.8
  2.5 0.1 copy.32
  2.6 0.7 pad_maximum_fusion.weight_ref
  3.3 0.0 copy-done
  3.3 0.6 gather_fusion
  4.0 0.6 pad_add_fusion.idx_ref
  4.6 72.2 %exchange.1.home_ref = bf16[2,8,256,128]{3,2,1,0:T(8,128)(2,1)} custom-call(s32[26]{0:T(128)} %pad_add_fusion.idx_ref, bf16[8,256,256]{2,1,0:T(8,128)(2,1)} %feat_ref.3, bf16[256,256]{1,0:T(8,128)(2,1)} %wqk_ref.1, bf16[256,256]{1,0:T(8,128)(2,1)} %wv_ref.1), custom_call_target="tpu_custom_call" | custom-call | tf_op jit(solution)/shard_map/exchange/pallas_call | solution.py:321
  76.8 12.8 %update.1 = bf16[8,256,256]{2,1,0:T(8,128)(2,1)} custom-call(f32[8,9]{1,0:T(8,128)} %pad_maximum_fusion.weight_ref, bf16[8,256,256]{2,1,0:T(8,128)(2,1)} %feat_ref.3, bf16[2,8,256,128]{3,2,1,0:T(8,128)(2,1)} %exchange.1.home_ref, bf16[256,256]{1,0:T(8,128)(2,1)} %wout_ref.1, bf16[512,512]{1,0:T(8,128)(2,1)} %wmi_ref.1, bf16[512,256]{1,0:T(8,128)(2,1)} %wmo_ref.1), custom_call_target="tpu_custom_call" | custom-call | tf_op jit(solution)/shard_map/update/pallas_call | solution.py:347
  (9 shorter events, 0.1 us)
Async XLA Ops:
  0.0 3.3 %copy-start = (s32[32]{0:T(128)S(1)}, s32[32]{0:T(128)}, u32[]{:S(2)}) copy-start(s32[32]{0:T(128)} %param.9) | copy-start | bytes 388
  0.0 0.7 copy-start.1

commit v2 on v1

v2 whole, which is shorter than its diff:
```python
import functools

import jax
import jax.numpy as jnp
from jax import lax
from jax.experimental import pallas as pl
from jax.experimental.pallas import tpu as pltpu
from jax.sharding import PartitionSpec as P

HEADS = 4
SLAB = 128
UNITS = 4
MESH = pl.DeviceIdType.MESH

ln_eps = 1e-05


def partner(me, step, n):
    if n & (n - 1):
        return lax.rem(me + step, n)
    peer = 0
    bit = 1
    while bit < n:
        mine = (me // bit) % 2
        peer = peer + ((mine + (step // bit) % 2) % 2) * bit
        bit *= 2
    return peer


def erf(x):
    x = jnp.clip(x, -3.832506856900711, 3.832506856900711)
    y = x * x
    top = jnp.float32(0.00022905065861350646)
    for c in (0.0034082910107109506, 0.050955695062380861, 0.18520832239976145, 1.128379143519084):
        top = top * y + jnp.float32(c)
    low = jnp.float32(-1.1791602954361697e-7)
    for c in (
        0.000023547966471313185,
        0.0010179625278914885,
        0.014070470171167667,
        0.11098505178285362,
        0.49746925110067538,
        1.0,
    ):
        low = low * y + jnp.float32(c)
    return x * top / low


def layer_kernel(
    dims,
    table_ref,
    counts_ref,
    feat_ref,
    wqk_ref,
    wv_ref,
    wout_ref,
    wmi_ref,
    wmo_ref,
    out_ref,
    *scratch,
):
    n_pair, n_sub, per_src, units, slabs, head_dim = dims
    img_grp, kp, width = feat_ref.shape
    positions = 2 * n_sub
    sources = n_pair * per_src
    points = n_sub * kp
    part = kp // units
    tile = n_sub * part
    scratch = list(scratch)
    take, pick, back, share = [scratch.pop(0) for _ in range(4)]
    send1, send2, qk, vx, msg, hsend, mean, hidden, active = [scratch.pop(0) for _ in range(9)]
    arrived = [scratch.pop(0) for _ in range(units)]
    rows_in = [scratch.pop(0) for _ in range(units)]
    returned = [scratch.pop(0) for _ in range(units)]
    home = [scratch.pop(0) for _ in range(units)]
    s1, r1, s2, r2, s3, r3, s4, r4 = scratch

    me_pair = lax.axis_index("pair")
    me_sub = lax.axis_index("sub")

    barrier = pltpu.get_barrier_semaphore()
    for step in range(1, n_pair):
        pl.semaphore_signal(
            barrier, inc=1, device_id={"pair": partner(me_pair, step, n_pair)}, device_id_type=MESH
        )
    for step in range(1, n_sub):
        pl.semaphore_signal(
            barrier, inc=1, device_id={"sub": partner(me_sub, step, n_sub)}, device_id_type=MESH
        )

    low_image = me_pair * img_grp
    zero = jnp.int32(0)

    def owner_tables(owner, uses):
        seen = zero
        chosen = [zero] * per_src
        for j in range(positions):
            image = table_ref[owner * positions + j] - low_image
            here = (image >= 0) & (image < img_grp)
            for r in range(per_src):
                chosen[r] = jnp.where(here & (seen == r), image, chosen[r])
            seen = seen + here.astype(jnp.int32)
        uses = list(uses)
        for r in range(per_src):
            take[owner * per_src + r] = chosen[r]
            for i in range(img_grp):
                hit = ((chosen[r] == i) & (seen > r)).astype(jnp.int32)
                share[i * sources + owner * per_src + r] = hit.astype(jnp.float32)
                uses[i] = uses[i] + hit
        return tuple(uses)

    uses = lax.fori_loop(0, n_pair, owner_tables, (zero,) * img_grp)
    divisor = [jnp.maximum(u, 1).astype(jnp.float32) for u in uses]

    for j in range(positions):
        pick[j] = zero

    def pick_tables(group, carry):
        seen = zero
        chosen = [zero] * per_src
        for j in range(positions):
            image = table_ref[me_pair * positions + j] - group * img_grp
            here = (image >= 0) & (image < img_grp)
            for r in range(per_src):
                chosen[r] = jnp.where(here & (seen == r), j, chosen[r])
            rank = jnp.minimum(seen, per_src - 1)
            pick[j] = jnp.where(here, group * per_src + rank, pick[j])
            seen = seen + here.astype(jnp.int32)
        for r in range(per_src):
            back[group * per_src + r] = chosen[r]
        return carry

    lax.fori_loop(0, n_pair, pick_tables, 0)
    slot_counts = [
        counts_ref[jnp.maximum(table_ref[me_pair * positions + 2 * me_sub + side], 0)]
        for side in range(2)
    ]

    pl.semaphore_wait(barrier, n_pair + n_sub - 2)

    waits = []
    pair_steps = list(range(n_pair - 1, 0, -1))
    sub_steps = list(range(n_sub - 1, 0, -1))

    def send(src, dst, send_sem, recv_sem, device):
        copy = pltpu.make_async_remote_copy(
            src_ref=src,
            dst_ref=dst,
            send_sem=send_sem,
            recv_sem=recv_sem,
            device_id=device,
            device_id_type=MESH,
        )
        copy.start()
        waits.append(copy)
        return copy

    phase1, phase2, phase3, phase4 = {}, {}, {}, {}
    mine1 = pl.ds(me_pair * per_src, per_src)
    for u in range(units):
        rows = pl.ds(u * part, part)
        for step in pair_steps:
            peer = partner(me_pair, step, n_pair)
            for r in range(per_src):
                send1[u, step, r] = feat_ref[take[peer * per_src + r], rows, :]
            phase1[u, step] = send(
                send1.at[u, step], arrived[u].at[mine1], s1.at[step, u], r1.at[step, u], {"pair": peer}
            )
    for u in range(units):
        rows = pl.ds(u * part, part)
        for r in range(per_src):
            own = me_pair * per_src + r
            arrived[u][own] = feat_ref[take[own], rows, :]

    for u in range(units):
        for step in pair_steps:
            phase1[u, step].wait_recv()
        for step in sub_steps:
            peer = partner(me_sub, step, n_sub)
            for side in range(2):
                send2[u, step, side] = arrived[u][pick[2 * peer + side]]
            phase2[u, step] = send(
                send2.at[u, step],
                rows_in[u].at[:, me_sub],
                s2.at[step, u],
                r2.at[step, u],
                {"sub": peer},
            )
        for side in range(2):
            rows_in[u][side, me_sub] = arrived[u][pick[2 * me_sub + side]]

    ones = jnp.ones((tile, SLAB), jnp.bfloat16)
    scale = head_dim ** (-0.5)
    in_slab = SLAB // head_dim
    tile_lane = lax.broadcasted_iota(jnp.int32, (tile, SLAB), 1) // head_dim

    for u in range(units):
        for step in sub_steps:
            phase2[u, step].wait_recv()
        where = pl.ds(u * tile, tile)
        for side in range(2):
            x = rows_in[u][side].reshape(tile, width)
            q = jnp.dot(x, wqk_ref[...], preferred_element_type=jnp.float32)
            qk[side, where, :] = q.astype(jnp.bfloat16)
            v = jnp.dot(x, wv_ref[...], preferred_element_type=jnp.float32).astype(jnp.bfloat16)
            for slab in range(slabs):
                vx[side, slab, where, :SLAB] = v[:, slab * SLAB : (slab + 1) * SLAB]
                vx[side, slab, where, SLAB:] = ones

    order = lax.broadcasted_iota(jnp.int32, (1, points), 1)
    col_ids = (order // part) % n_sub * kp + order // tile * part + order % part

    def attend(u, side):
        other = 1 - side
        valid = col_ids < slot_counts[other]
        for slab in range(slabs):
            columns = slice(slab * SLAB, (slab + 1) * SLAB)
            q = qk[side, pl.ds(u * tile, tile), columns] * jnp.asarray(scale, jnp.bfloat16)
            out = jnp.zeros((tile, SLAB), jnp.float32)
            for head in range(in_slab):
                mine = tile_lane == head
                qh = jnp.where(mine, q, jnp.zeros_like(q))
                sim = lax.dot_general(
                    qh,
                    qk[other, :, columns],
                    (((1,), (1,)), ((), ())),
                    preferred_element_type=jnp.float32,
                )
                sim = jnp.where(valid, sim, -jnp.inf)
                top = jnp.max(sim, axis=1, keepdims=True)
                weight = jnp.exp(sim - top).astype(jnp.bfloat16)
                both = jnp.dot(weight, vx[other, slab], preferred_element_type=jnp.float32)
                out = jnp.where(mine, both[:, :SLAB] / both[:, SLAB:], out)
            msg[u, side, :, :, columns] = out.astype(jnp.bfloat16).reshape(n_sub, part, SLAB)

    def give_back(u, side):
        for step in sub_steps:
            peer = partner(me_sub, step, n_sub)
            phase3[u, side, step] = send(
                msg.at[u, side, peer],
                returned[u].at[2 * me_sub + side],
                s3.at[step, u, side],
                r3.at[step, u, side],
                {"sub": peer},
            )
        returned[u][2 * me_sub + side] = msg[u, side, me_sub]

    def send_home(u):
        for side in range(2):
            for step in sub_steps:
                phase3[u, side, step].wait_recv()
        for step in pair_steps:
            peer = partner(me_pair, step, n_pair)
            for r in range(per_src):
                hsend[u, step, r] = returned[u][back[peer * per_src + r]]
            phase4[u, step] = send(
                hsend.at[u, step], home[u].at[mine1], s4.at[step, u], r4.at[step, u], {"pair": peer}
            )
        for r in range(per_src):
            own = me_pair * per_src + r
            home[u][own] = returned[u][back[own]]

    block = img_grp * part
    strip = 32 if block % 32 == 0 else 16

    def update(u):
        for step in pair_steps:
            phase4[u, step].wait_recv()
        for i in range(img_grp):
            total = jnp.zeros((part, width), jnp.float32)
            for s in range(sources):
                total = total + home[u][s].astype(jnp.float32) * share[i * sources + s]
            mean[pl.ds(i * part, part), :] = (total / divisor[i]).astype(jnp.bfloat16)
        lifted = jnp.dot(mean[...], wout_ref[...], preferred_element_type=jnp.float32)
        feat = feat_ref[:, pl.ds(u * part, part), :].reshape(block, width)
        hidden[...] = jnp.dot(
            feat, wmi_ref[:width, :], preferred_element_type=jnp.float32
        ) + jnp.dot(
            lifted.astype(jnp.bfloat16), wmi_ref[width:, :], preferred_element_type=jnp.float32
        )

        def strip_body(t, carry):
            rows = pl.ds(pl.multiple_of(t * strip, strip), strip)
            h = hidden[rows, :]
            centered = h - jnp.mean(h, axis=-1, keepdims=True)
            variance = jnp.mean(centered * centered, axis=-1, keepdims=True)
            normed = centered * lax.rsqrt(variance + ln_eps)
            gelu = 0.5 * normed * (1.0 + erf(normed * (0.5**0.5)))
            active[rows, :] = gelu.astype(jnp.bfloat16)
            return carry

        lax.fori_loop(0, block // strip, strip_body, 0, unroll=2)
        out = feat.astype(jnp.float32) + jnp.dot(
            active[...], wmo_ref[...], preferred_element_type=jnp.float32
        )
        out_ref[:, pl.ds(u * part, part), :] = out.astype(jnp.bfloat16).reshape(
            img_grp, part, width
        )

    lag = 2
    for u in range(units + lag + 1):
        if u < units:
            for side in range(2):
                attend(u, side)
                give_back(u, side)
        if 0 <= u - lag < units:
            send_home(u - lag)
        if 0 <= u - lag - 1 < units:
            update(u - lag - 1)
    for copy in waits:
        copy.wait_send()


def local(features, counts, pair_table, w_qk, w_value, w_out, w_merge_in, w_merge_out):
    n_pair = lax.axis_size("pair")
    n_sub = lax.axis_size("sub")
    img_grp, kp, width = features.shape
    hidden_width = w_merge_in.shape[1]
    per_src = 2 * n_sub // n_pair
    positions = 2 * n_sub
    sources = n_pair * per_src
    slabs = width // SLAB
    points = n_sub * kp
    units = UNITS
    part = kp // units
    bf = jnp.bfloat16
    dma = pltpu.SemaphoreType.DMA
    vmem = pl.BlockSpec(memory_space=pltpu.VMEM)
    smem = pl.BlockSpec(memory_space=pltpu.SMEM)
    dims = (n_pair, n_sub, per_src, units, slabs, width // HEADS)
    return pl.pallas_call(
        functools.partial(layer_kernel, dims),
        out_shape=jax.ShapeDtypeStruct(features.shape, bf),
        in_specs=[smem, smem] + [vmem] * 6,
        out_specs=vmem,
        scratch_shapes=[
            pltpu.SMEM((sources,), jnp.int32),
            pltpu.SMEM((positions,), jnp.int32),
            pltpu.SMEM((sources,), jnp.int32),
            pltpu.SMEM((img_grp * sources,), jnp.float32),
            pltpu.VMEM((units, n_pair, per_src, part, width), bf),
            pltpu.VMEM((units, n_sub, 2, part, width), bf),
            pltpu.VMEM((2, points, width), bf),
            pltpu.VMEM((2, slabs, points, 2 * SLAB), bf),
            pltpu.VMEM((units, 2, n_sub, part, width), bf),
            pltpu.VMEM((units, n_pair, per_src, part, width), bf),
            pltpu.VMEM((img_grp * part, width), bf),
            pltpu.VMEM((img_grp * part, hidden_width), jnp.float32),
            pltpu.VMEM((img_grp * part, hidden_width), bf),
        ]
        + [pltpu.VMEM((sources, part, width), bf) for _ in range(units)]
        + [pltpu.VMEM((2, n_sub, part, width), bf) for _ in range(units)]
        + [pltpu.VMEM((positions, part, width), bf) for _ in range(units)]
        + [pltpu.VMEM((sources, part, width), bf) for _ in range(units)]
        + [dma((n_pair, units))] * 2
        + [dma((n_sub, units))] * 2
        + [dma((n_sub, units, 2))] * 2
        + [dma((n_pair, units))] * 2,
        compiler_params=pltpu.CompilerParams(
            collective_id=0, has_side_effects=True, vmem_limit_bytes=56 * 1024 * 1024
        ),
        name="layer",
    )(
        pair_table.reshape(-1),
        counts,
        features,
        w_qk,
        w_value,
        w_out,
        w_merge_in,
        w_merge_out,
    )


def solution(mesh):
    in_specs = (
        P(("parts", "pair"), "sub", None),
        P("parts"),
        P("parts", None, None),
        P(),
        P(),
        P(),
        P(),
        P(),
    )
    out_specs = P(("parts", "pair"), "sub", None)
    return jax.shard_map(local, mesh=mesh, in_specs=in_specs, out_specs=out_specs, check_vma=False)
```

time: 89.9 us -> 76.2 us (0.85)
  Pallas kernels: 85.1 us -> 72.3 us
  other arithmetic: 2.45 us -> 0 us
  local copies, waits for them, and re-layouts: 2.06 us -> 3.66 us
    pallas_call x2 -> x1, Pallas kernels: 85.1 us -> 72.3 us  [local(): pl.pallas_call(functools.partial(layer_kernel, dims), out_shape=jax.Shape...]
    unnamed x5 -> x2, local copies, waits for them, and re-layouts: 0.79 us -> 3.05 us
    concatenate x2 -> x0, other arithmetic: 1.26 us -> none  [the longest x1 0.67 us: local(): weights = jnp.concatenate([hot, uses], axis=1)]
where the time goes in v2:
time: 76.2 us; the launch traced here: 76 us
  Pallas kernels  72.3 us (95%)
  local copies, waits for them, and re-layouts  3.66 us (5%)
    pallas_call x1, Pallas kernels, local(): pl.pallas_call(functools.partial(layer_kernel, dims), out_shape=jax.Shape...  72.3 us
    unnamed x2, local copies, waits for them, and re-layouts  3.05 us

profile of v2, /device:TPU:0, one launch (start us, length us, event | category | flops | bytes accessed | tf_op | source)
XLA Modules:
  0.0 76.0 jit_solution(1631592789218843784)
XLA Ops:
  0.0 0.8 %copy.10 = s32[4,4,2]{2,1,0:T(4,128)S(1)} copy(s32[4,4,2]{1,2,0:T(2,128)} %param.10) | data formatting | bytes 256 | tf_op args[2]
  0.8 0.6 reshape.3.table_ref
  1.4 72.3 %layer.1 = bf16[8,256,256]{2,1,0:T(8,128)(2,1)} custom-call(s32[32]{0:T(128)} %reshape.3.table_ref, s32[32]{0:T(128)} %counts_ref.1, bf16[8,256,256]{2,1,0:T(8,128)(2,1)} %feat_ref.1, bf16[256,256]{1,0:T(8,128)(2,1)} %wqk_ref.1, bf16[256,256]{1,0:T(8,128)(2,1)} %wv_ref.1, bf16[256,256]{1,0:T(8,128)(2,1)} %wout_ref.1, bf16[512,512]{1,0:T(8,128)(2,1)} %wmi_ref.1, ...), custom_call_target="tpu_custom_call" | custom-call | tf_op jit(solution)/shard_map/layer/pallas_call | solution.py:331
  73.7 2.3 %copy.12 = bf16[8,256,256]{2,1,0:T(8,128)(2,1)} copy(bf16[8,256,256]{2,1,0:T(8,128)(2,1)} %layer.1) | data formatting | bytes 2097152

commit v3 on v2

--- a/solution.py
+++ b/solution.py
@@ -51,11 +51,11 @@
     table_ref,
     counts_ref,
     feat_ref,
-    wqk_ref,
-    wv_ref,
-    wout_ref,
-    wmi_ref,
-    wmo_ref,
+    wqk_hbm,
+    wv_hbm,
+    wout_hbm,
+    wmi_hbm,
+    wmo_hbm,
     out_ref,
     *scratch,
 ):
@@ -67,8 +67,9 @@
     part = kp // units
     tile = n_sub * part
     scratch = list(scratch)
-    take, pick, back, share = [scratch.pop(0) for _ in range(4)]
+    take, held, pick, back, share = [scratch.pop(0) for _ in range(5)]
     send1, send2, qk, vx, msg, hsend, mean, hidden, active = [scratch.pop(0) for _ in range(9)]
+    wqk_ref, wv_ref, wout_ref, wmi_ref, wmo_ref, wsem = [scratch.pop(0) for _ in range(6)]
     arrived = [scratch.pop(0) for _ in range(units)]
     rows_in = [scratch.pop(0) for _ in range(units)]
     returned = [scratch.pop(0) for _ in range(units)]
@@ -78,6 +79,18 @@
     me_pair = lax.axis_index("pair")
     me_sub = lax.axis_index("sub")
 
+    weights = [
+        pltpu.make_async_copy(src, dst, wsem.at[n])
+        for n, (src, dst) in enumerate(
+            (
+                (wqk_hbm, wqk_ref),
+                (wv_hbm, wv_ref),
+                (wout_hbm, wout_ref),
+                (wmi_hbm, wmi_ref),
+                (wmo_hbm, wmo_ref),
+            )
+        )
+    ]
     barrier = pltpu.get_barrier_semaphore()
     for step in range(1, n_pair):
         pl.semaphore_signal(
@@ -91,53 +104,24 @@
     low_image = me_pair * img_grp
     zero = jnp.int32(0)
 
-    def owner_tables(owner, uses):
+    def send_table(owner, carry):
         seen = zero
         chosen = [zero] * per_src
         for j in range(positions):
-            image = table_ref[owner * positions + j] - low_image
+            image = table_ref[owner, j // 2, j % 2] - low_image
             here = (image >= 0) & (image < img_grp)
             for r in range(per_src):
                 chosen[r] = jnp.where(here & (seen == r), image, chosen[r])
             seen = seen + here.astype(jnp.int32)
-        uses = list(uses)
         for r in range(per_src):
             take[owner * per_src + r] = chosen[r]
-            for i in range(img_grp):
-                hit = ((chosen[r] == i) & (seen > r)).astype(jnp.int32)
-                share[i * sources + owner * per_src + r] = hit.astype(jnp.float32)
-                uses[i] = uses[i] + hit
-        return tuple(uses)
-
-    uses = lax.fori_loop(0, n_pair, owner_tables, (zero,) * img_grp)
-    divisor = [jnp.maximum(u, 1).astype(jnp.float32) for u in uses]
-
-    for j in range(positions):
-        pick[j] = zero
-
-    def pick_tables(group, carry):
-        seen = zero
-        chosen = [zero] * per_src
-        for j in range(positions):
-            image = table_ref[me_pair * positions + j] - group * img_grp
-            here = (image >= 0) & (image < img_grp)
-            for r in range(per_src):
-                chosen[r] = jnp.where(here & (seen == r), j, chosen[r])
-            rank = jnp.minimum(seen, per_src - 1)
-            pick[j] = jnp.where(here, group * per_src + rank, pick[j])
-            seen = seen + here.astype(jnp.int32)
-        for r in range(per_src):
-            back[group * per_src + r] = chosen[r]
+            held[owner * per_src + r] = jnp.where(seen > r, chosen[r], -1)
         return carry
 
-    lax.fori_loop(0, n_pair, pick_tables, 0)
-    slot_counts = [
-        counts_ref[jnp.maximum(table_ref[me_pair * positions + 2 * me_sub + side], 0)]
-        for side in range(2)
-    ]
-
+    lax.fori_loop(0, n_pair, send_table, 0)
     pl.semaphore_wait(barrier, n_pair + n_sub - 2)
-
+    for copy in weights:
+        copy.start()
     waits = []
     pair_steps = list(range(n_pair - 1, 0, -1))
     sub_steps = list(range(n_sub - 1, 0, -1))
@@ -172,6 +156,41 @@
             own = me_pair * per_src + r
             arrived[u][own] = feat_ref[take[own], rows, :]
 
+    for j in range(positions):
+        pick[j] = zero
+
+    def pick_tables(group, carry):
+        seen = zero
+        chosen = [zero] * per_src
+        for j in range(positions):
+            image = table_ref[me_pair, j // 2, j % 2] - group * img_grp
+            here = (image >= 0) & (image < img_grp)
+            for r in range(per_src):
+                chosen[r] = jnp.where(here & (seen == r), j, chosen[r])
+            rank = jnp.minimum(seen, per_src - 1)
+            pick[j] = jnp.where(here, group * per_src + rank, pick[j])
+            seen = seen + here.astype(jnp.int32)
+        for r in range(per_src):
+            back[group * per_src + r] = chosen[r]
+        return carry
+
+    lax.fori_loop(0, n_pair, pick_tables, 0)
+    slot_counts = [
+        counts_ref[jnp.maximum(table_ref[me_pair, me_sub, side], 0)]
+        for side in range(2)
+    ]
+
+    def share_table(s, uses):
+        uses = list(uses)
+        for i in range(img_grp):
+            hit = (held[s] == i).astype(jnp.int32)
+            share[i * sources + s] = hit.astype(jnp.float32)
+            uses[i] = uses[i] + hit
+        return tuple(uses)
+
+    uses = lax.fori_loop(0, sources, share_table, (zero,) * img_grp)
+    divisor = [jnp.maximum(u, 1).astype(jnp.float32) for u in uses]
+
     for u in range(units):
         for step in pair_steps:
             phase1[u, step].wait_recv()
@@ -189,6 +208,8 @@
         for side in range(2):
             rows_in[u][side, me_sub] = arrived[u][pick[2 * me_sub + side]]
 
+    weights[0].wait()
+    weights[1].wait()
     ones = jnp.ones((tile, SLAB), jnp.bfloat16)
     scale = head_dim ** (-0.5)
     in_slab = SLAB // head_dim
@@ -261,9 +282,11 @@
             home[u][own] = returned[u][back[own]]
 
     block = img_grp * part
-    strip = 32 if block % 32 == 0 else 16
+    strip = block // 2
 
     def update(u):
+        feat = feat_ref[:, pl.ds(u * part, part), :].reshape(block, width)
+        hidden[...] = jnp.dot(feat, wmi_ref[:width, :], preferred_element_type=jnp.float32)
         for step in pair_steps:
             phase4[u, step].wait_recv()
         for i in range(img_grp):
@@ -272,10 +295,7 @@
                 total = total + home[u][s].astype(jnp.float32) * share[i * sources + s]
             mean[pl.ds(i * part, part), :] = (total / divisor[i]).astype(jnp.bfloat16)
         lifted = jnp.dot(mean[...], wout_ref[...], preferred_element_type=jnp.float32)
-        feat = feat_ref[:, pl.ds(u * part, part), :].reshape(block, width)
-        hidden[...] = jnp.dot(
-            feat, wmi_ref[:width, :], preferred_element_type=jnp.float32
-        ) + jnp.dot(
+        hidden[...] = hidden[...] + jnp.dot(
             lifted.astype(jnp.bfloat16), wmi_ref[width:, :], preferred_element_type=jnp.float32
         )
 
@@ -289,7 +309,7 @@
             active[rows, :] = gelu.astype(jnp.bfloat16)
             return carry
 
-        lax.fori_loop(0, block // strip, strip_body, 0, unroll=2)
+        lax.fori_loop(0, block // strip, strip_body, 0)
         out = feat.astype(jnp.float32) + jnp.dot(
             active[...], wmo_ref[...], preferred_element_type=jnp.float32
         )
@@ -297,6 +317,8 @@
             img_grp, part, width
         )
 
+    for copy in weights[2:]:
+        copy.wait()
     lag = 2
     for u in range(units + lag + 1):
         if u < units:
@@ -321,7 +343,7 @@
     sources = n_pair * per_src
     slabs = width // SLAB
     points = n_sub * kp
-    units = UNITS
+    units = min(UNITS, kp // 16)
     part = kp // units
     bf = jnp.bfloat16
     dma = pltpu.SemaphoreType.DMA
@@ -331,9 +353,10 @@
     return pl.pallas_call(
         functools.partial(layer_kernel, dims),
         out_shape=jax.ShapeDtypeStruct(features.shape, bf),
-        in_specs=[smem, smem] + [vmem] * 6,
+        in_specs=[smem, smem, vmem] + [pl.BlockSpec(memory_space=pl.ANY)] * 5,
         out_specs=vmem,
         scratch_shapes=[
+            pltpu.SMEM((sources,), jnp.int32),
             pltpu.SMEM((sources,), jnp.int32),
             pltpu.SMEM((positions,), jnp.int32),
             pltpu.SMEM((sources,), jnp.int32),
@@ -348,6 +371,10 @@
             pltpu.VMEM((img_grp * part, hidden_width), jnp.float32),
             pltpu.VMEM((img_grp * part, hidden_width), bf),
         ]
+        + [pltpu.VMEM(w.shape, bf) for w in (w_qk, w_value, w_out, w_merge_in, w_merge_out)]
+        + [
+            dma((5,)),
+        ]
         + [pltpu.VMEM((sources, part, width), bf) for _ in range(units)]
         + [pltpu.VMEM((2, n_sub, part, width), bf) for _ in range(units)]
         + [pltpu.VMEM((positions, part, width), bf) for _ in range(units)]
@@ -361,7 +388,7 @@
         ),
         name="layer",
     )(
-        pair_table.reshape(-1),
+        pair_table,
         counts,
         features,
         w_qk,

time: 76.2 us -> 74.2 us (0.974)
  Pallas kernels: 72.3 us -> 70.4 us
    pallas_call x1, Pallas kernels: 72.3 us -> 70.4 us  [local(): pl.pallas_call(functools.partial(layer_kernel, dims), out_shape=jax.Shape...]
where the time goes in v3:
time: 74.2 us; the launch traced here: 74 us
  Pallas kernels  70.4 us (95%)
  local copies, waits for them, and re-layouts  3.64 us (5%)
    pallas_call x1, Pallas kernels, local(): pl.pallas_call(functools.partial(layer_kernel, dims), out_shape=jax.Shape...  70.4 us
    unnamed x2, local copies, waits for them, and re-layouts  3.64 us

profile of v3, /device:TPU:0, one launch (start us, length us, event | category | flops | bytes accessed | tf_op | source)
XLA Modules:
  0.0 74.0 jit_solution(4828959633135737668)
XLA Ops:
  0.0 1.4 %copy.9.table_ref = s32[4,4,2]{2,1,0:T(4,128)} copy(s32[4,4,2]{1,2,0:T(2,128)} %param.10) | data formatting | bytes 256 | tf_op args[2]
  1.4 70.4 %layer.1 = bf16[8,256,256]{2,1,0:T(8,128)(2,1)} custom-call(s32[4,4,2]{2,1,0:T(4,128)} %copy.9.table_ref, s32[32]{0:T(128)} %counts_ref.1, bf16[8,256,256]{2,1,0:T(8,128)(2,1)} %feat_ref.1, bf16[256,256]{1,0:T(8,128)(2,1)} %wqk_hbm.1, bf16[256,256]{1,0:T(8,128)(2,1)} %wv_hbm.1, bf16[256,256]{1,0:T(8,128)(2,1)} %wout_hbm.1, bf16[512,512]{1,0:T(8,128)(2,1)} %wmi_hbm.1, ...), custom_call_target="tpu_custom_call" | custom-call | tf_op jit(solution)/shard_map/layer/pallas_call | solution.py:353
  71.7 2.3 %copy.11 = bf16[8,256,256]{2,1,0:T(8,128)(2,1)} copy(bf16[8,256,256]{2,1,0:T(8,128)(2,1)} %layer.1) | data formatting | bytes 2097152

commit v4 on v3

--- a/solution.py
+++ b/solution.py
@@ -108,7 +108,7 @@
         seen = zero
         chosen = [zero] * per_src
         for j in range(positions):
-            image = table_ref[owner, j // 2, j % 2] - low_image
+            image = table_ref[owner, j % 2, j // 2] - low_image
             here = (image >= 0) & (image < img_grp)
             for r in range(per_src):
                 chosen[r] = jnp.where(here & (seen == r), image, chosen[r])
@@ -163,7 +163,7 @@
         seen = zero
         chosen = [zero] * per_src
         for j in range(positions):
-            image = table_ref[me_pair, j // 2, j % 2] - group * img_grp
+            image = table_ref[me_pair, j % 2, j // 2] - group * img_grp
             here = (image >= 0) & (image < img_grp)
             for r in range(per_src):
                 chosen[r] = jnp.where(here & (seen == r), j, chosen[r])
@@ -176,7 +176,7 @@
 
     lax.fori_loop(0, n_pair, pick_tables, 0)
     slot_counts = [
-        counts_ref[jnp.maximum(table_ref[me_pair, me_sub, side], 0)]
+        counts_ref[jnp.maximum(table_ref[me_pair, side, me_sub], 0)]
         for side in range(2)
     ]
 
@@ -388,7 +388,7 @@
         ),
         name="layer",
     )(
-        pair_table,
+        jnp.swapaxes(pair_table, 1, 2),
         counts,
         features,
         w_qk,

time: 74.2 us -> 72.8 us (0.981)
  local copies, waits for them, and re-layouts: 3.64 us -> 2.26 us
    unnamed x2 -> x1, local copies, waits for them, and re-layouts: 3.64 us -> 2.26 us
where the time goes in v4:
time: 72.8 us; the launch traced here: 72.6 us
  Pallas kernels  70.4 us (97%)
  local copies, waits for them, and re-layouts  2.26 us (3%)
    pallas_call x1, Pallas kernels, local(): pl.pallas_call(functools.partial(layer_kernel, dims), out_shape=jax.Shape...  70.4 us
    unnamed x1, local copies, waits for them, and re-layouts  2.26 us

profile of v4, /device:TPU:0, one launch (start us, length us, event | category | flops | bytes accessed | tf_op | source)
XLA Modules:
  0.0 72.6 jit_solution(16265371704651906392)
XLA Ops:
  0.0 70.4 %layer.1 = bf16[8,256,256]{2,1,0:T(8,128)(2,1)} custom-call(s32[4,2,4]{2,1,0:T(2,128)} %bitcast.1, s32[32]{0:T(128)} %counts_ref.1, bf16[8,256,256]{2,1,0:T(8,128)(2,1)} %feat_ref.1, bf16[256,256]{1,0:T(8,128)(2,1)} %wqk_hbm.1, bf16[256,256]{1,0:T(8,128)(2,1)} %wv_hbm.1, bf16[256,256]{1,0:T(8,128)(2,1)} %wout_hbm.1, bf16[512,512]{1,0:T(8,128)(2,1)} %wmi_hbm.1, ...), custom_call_target="tpu_custom_call" | custom-call | tf_op jit(solution)/shard_map/layer/pallas_call | solution.py:353
  70.4 2.3 %copy.10 = bf16[8,256,256]{2,1,0:T(8,128)(2,1)} copy(bf16[8,256,256]{2,1,0:T(8,128)(2,1)} %layer.1) | data formatting | bytes 2097152
